TPU v7x, 32 devices: a whole 2x2x4 slice. The times are simulated.
32 devices in a mesh: group: 2 (over x), expert: 8 (over z, y), cuts: 2 (over core).
Axes of the slice: x: 2, y: 2, z: 4, core: 2. Of those that a mesh axis runs over, the one named last changes fastest.
Arguments:
- x_in: bfloat16 [512, 4096], P(('group', 'expert'), 'cuts'), parts along dimension 0, may hold values from -6 to 6
- routes: int32 [512, 2], P(('group', 'expert')), parts along dimension 0, may hold values from 0 to 15, as said below
- conv_state: float32 [64, 3, 4096], P('group', None, ('expert', 'cuts')), parts along dimension 0, may hold values from -6 to 6
- ssm_state: float32 [64, 16, 4096], P('group', None, ('expert', 'cuts')), parts along dimension 0, may hold values from -6 to 6
- mamba_gain: float32 [4096], replicated, may hold values from 0.1 to 1.9
- in_x: bfloat16 [4096, 4096], P(None, ('expert', 'cuts')), may hold values from -0.09375 to 0.09375
- in_z: bfloat16 [4096, 4096], P(None, ('expert', 'cuts')), may hold values from -0.09375 to 0.09375
- conv_w: float32 [4, 4096], P(None, ('expert', 'cuts')), may hold values from -3 to 3
- conv_b: float32 [4096], P(('expert', 'cuts')), may hold values from -3 to 3
- xproj_dt: bfloat16 [4096, 512], P(('expert', 'cuts')), may hold values from -0.09375 to 0.09375
- xproj_bc: bfloat16 [4096, 32], P(('expert', 'cuts')), may hold values from -0.09375 to 0.09375
- dt_proj: bfloat16 [512, 4096], P(None, ('expert', 'cuts')), may hold values from -0.25 to 0.25
- dt_bias: float32 [4096], P(('expert', 'cuts')), may hold values from -4 to 0
- a_rate: float32 [16, 4096], P(None, ('expert', 'cuts')), may hold values from 0.5 to 16
- d_skip: float32 [4096], P(('expert', 'cuts')), may hold values from 0.5 to 1.5
- out_proj: bfloat16 [4096, 4096], P(('expert', 'cuts')), may hold values from -0.09375 to 0.09375
- moe_gain: float32 [4096], replicated, may hold values from 0.1 to 1.9
- router: bfloat16 [4096, 16], replicated, may hold values from -0.09375 to 0.09375
- w_gate: bfloat16 [4096, 12288], P(None, ('expert', 'cuts')), may hold values from -0.09375 to 0.09375
- w_up: bfloat16 [4096, 12288], P(None, ('expert', 'cuts')), may hold values from -0.09375 to 0.09375
- w_down: bfloat16 [12288, 4096], P(('expert', 'cuts')), may hold values from -0.078125 to 0.078125
Outputs:
- stream_out: bfloat16 [512, 4096], P(('group', 'expert'), 'cuts'), parts along dimension 0
- new_state: float32 [64, 16, 4096], P('group', None, ('expert', 'cuts')), parts along dimension 0
There are 2 independent parts, one for each index of `group`. A program takes and returns all parts, laid end to end along the dimension named above; an argument that names none is the same for every part. Nothing has to cross between parts.
Inputs may be any that keep to these rules, and one draw needn't show every extreme that they name: `routes`: each token names 2 different experts. Among the 32 tokens of one index of expert (aligned blocks of rows), at most 16 name any one expert below 2, and in every block one of them is named by exactly 16; no token names two experts below 2.
All inputs are finite; a program needn't handle non-finite values.
Results may differ from a plain program's by a relative error of at most 0.0095.
Values may be sent and summed in bfloat16 or wider, within the bound.
No kernel may reach another device: no remote copies, remote signals or barrier semaphores. Data moves between devices by JAX's collectives and lax.ppermute only.
A program may use at most 128 MiB of HBM per device.

v0:
```python
import jax
import jax.numpy as jnp
from jax import lax
from jax.sharding import PartitionSpec as P

EXPERTS = 2
DRAFT = 8
CAP = 16


def rms_norm(values, gain):
    values = values.astype(jnp.float32)
    scale = lax.rsqrt(jnp.mean(values * values, axis=-1, keepdims=True) + 1e-05)
    return (values * scale * gain).astype(jnp.bfloat16)


def ssm_steps(inputs, steps, b_maps, c_maps, state, a_rate, d_skip):
    outputs = []
    for place in range(inputs.shape[1]):
        decay = jnp.exp(-steps[:, place, None, :] * a_rate[None])
        state = (
            decay * state
            + (steps[:, place] * inputs[:, place])[:, None, :] * b_maps[:, place, :, None]
        )
        outputs.append(
            jnp.sum(c_maps[:, place, :, None] * state, axis=1) + d_skip * inputs[:, place]
        )
    return (jnp.stack(outputs, axis=1), state)


def on_device(
    x_in,
    routes,
    conv_state,
    ssm_state,
    mamba_gain,
    in_x,
    in_z,
    conv_w,
    conv_b,
    xproj_dt,
    xproj_bc,
    dt_proj,
    dt_bias,
    a_rate,
    d_skip,
    out_proj,
    moe_gain,
    router,
    w_gate,
    w_up,
    w_down,
):
    tok_count, half_width = x_in.shape
    requests = conv_state.shape[0]
    channels = in_x.shape[1]
    states = a_rate.shape[0]
    topk = routes.shape[1]
    owners = lax.axis_size("expert")
    pieces = lax.axis_size("cuts")
    full_x = lax.all_gather(x_in, "cuts", axis=1, tiled=True)
    normed = rms_norm(lax.all_gather(full_x, "expert", axis=0, tiled=True), mamba_gain)
    upper = jnp.dot(normed, in_x, preferred_element_type=jnp.float32)
    lower = jnp.dot(normed, in_z, preferred_element_type=jnp.float32)
    both = jnp.stack([upper, lower])
    u_pre = both[0]
    z_gate = both[1]
    seq = jnp.concatenate([conv_state, u_pre.reshape(requests, DRAFT, channels)], axis=1)
    conv = jnp.zeros((requests, DRAFT, channels), jnp.float32) + conv_b
    for tap in range(conv_w.shape[0]):
        conv = conv + conv_w[tap] * seq[:, tap : tap + DRAFT]
    u_act = jax.nn.silu(conv).astype(jnp.bfloat16)
    flat_u = u_act.reshape(requests * DRAFT, channels)
    dt_part = jnp.dot(flat_u, xproj_dt, preferred_element_type=jnp.float32)
    map_part = jnp.dot(flat_u, xproj_bc, preferred_element_type=jnp.float32)
    dt_low, maps = lax.psum((dt_part, map_part), ("expert", "cuts"))
    steps = jax.nn.softplus(
        jnp.dot(dt_low.astype(jnp.bfloat16), dt_proj, preferred_element_type=jnp.float32) + dt_bias
    )
    b_maps = maps[:, :states].reshape(requests, DRAFT, states)
    c_maps = maps[:, states:].reshape(requests, DRAFT, states)
    outputs, new_state = ssm_steps(
        u_act.astype(jnp.float32),
        steps.reshape(requests, DRAFT, channels),
        b_maps,
        c_maps,
        ssm_state,
        a_rate,
        d_skip,
    )
    gated = (outputs.reshape(requests * DRAFT, channels) * jax.nn.silu(z_gate)).astype(jnp.bfloat16)
    term = jnp.einsum(
        "etc,ckf->ektf",
        gated.reshape(owners, tok_count, channels),
        out_proj.reshape(channels, pieces, half_width),
        preferred_element_type=jnp.float32,
    )
    term = term.reshape(owners * pieces * tok_count, half_width)
    mixed_half = lax.psum_scatter(term, ("expert", "cuts"), scatter_dimension=0, tiled=True)
    stream_half = (x_in.astype(jnp.float32) + mixed_half).astype(jnp.bfloat16)
    stream = lax.all_gather(stream_half, "cuts", axis=1, tiled=True)
    normed2 = rms_norm(stream, moe_gain)
    logits = jnp.dot(normed2, router, preferred_element_type=jnp.float32)
    all_labels = jnp.arange(router.shape[1], dtype=jnp.int32)
    pick = (routes[:, :, None] == all_labels).astype(jnp.float32)
    chosen = jnp.sum(logits[:, None, :] * pick, axis=-1)
    weight0 = jax.nn.sigmoid(chosen[:, 0] - chosen[:, 1])
    labels = jnp.arange(EXPERTS, dtype=jnp.int32)
    flat_routes = routes.reshape(tok_count * topk)
    onehot = (flat_routes[:, None] == labels).astype(jnp.int32)
    rank = jnp.cumsum(onehot, axis=0) - 1
    slot = jnp.sum(rank * onehot, axis=-1)
    inside = jnp.sum(onehot, axis=-1)
    dest = jnp.where(inside > 0, flat_routes * CAP + slot, EXPERTS * CAP)
    row_width = normed2.shape[1]
    rows = jnp.repeat(normed2, topk, axis=0)
    buffer = (
        jnp.zeros((EXPERTS * CAP + 1, row_width), jnp.bfloat16).at[dest].set(rows)[: EXPERTS * CAP]
    )
    buffer = buffer.reshape(EXPERTS, CAP, row_width)
    holders = owners // EXPERTS
    outgoing = jnp.repeat(buffer, holders, axis=0)[:, None]
    received = lax.all_to_all(outgoing, "expert", split_axis=0, concat_axis=1, tiled=True)
    local, sources, count, features = received.shape
    tokens = received.reshape(local * sources * count, features)
    gate = jnp.dot(tokens, w_gate, preferred_element_type=jnp.float32)
    upval = jnp.dot(tokens, w_up, preferred_element_type=jnp.float32)
    act = (jax.nn.silu(gate) * upval).astype(jnp.bfloat16)
    partial_out = jnp.dot(act, w_down, preferred_element_type=jnp.float32)
    partial_out = partial_out.reshape(local, sources, count, features)
    returned = lax.all_to_all(
        partial_out.astype(jnp.bfloat16), "expert", split_axis=1, concat_axis=0, tiled=True
    ).astype(partial_out.dtype)
    back_width = returned.shape[3]
    grouped = jnp.sum(returned.reshape(EXPERTS, holders, CAP, back_width), axis=1).reshape(
        EXPERTS * CAP, back_width
    )
    table = jnp.concatenate([grouped, jnp.zeros((1, back_width), jnp.float32)], axis=0)
    picked = table[dest].reshape(tok_count, topk, back_width)
    expert_out = lax.psum_scatter(
        picked.astype(jnp.bfloat16), "cuts", scatter_dimension=2, tiled=True
    )
    expert_out = expert_out.astype(jnp.float32)
    total = (
        stream_half.astype(jnp.float32)
        + weight0[:, None] * expert_out[:, 0]
        + (1.0 - weight0)[:, None] * expert_out[:, 1]
    )
    return (total.astype(jnp.bfloat16), new_state)


def solution(mesh):
    return jax.shard_map(
        on_device,
        mesh=mesh,
        in_specs=(
            P(("group", "expert"), "cuts"),
            P(("group", "expert"), None),
            P("group", None, ("expert", "cuts")),
            P("group", None, ("expert", "cuts")),
            P(),
            P(None, ("expert", "cuts")),
            P(None, ("expert", "cuts")),
            P(None, ("expert", "cuts")),
            P(("expert", "cuts")),
            P(("expert", "cuts"), None),
            P(("expert", "cuts"), None),
            P(None, ("expert", "cuts")),
            P(("expert", "cuts")),
            P(None, ("expert", "cuts")),
            P(("expert", "cuts")),
            P(("expert", "cuts"), None),
            P(),
            P(),
            P(None, ("expert", "cuts")),
            P(None, ("expert", "cuts")),
            P(("expert", "cuts"), None),
        ),
        out_specs=(P(("group", "expert"), "cuts"), P("group", None, ("expert", "cuts"))),
        check_vma=False,
    )
```

profile of v0, /device:TPU:0, one launch (start us, length us, event | category | flops | bytes accessed | tf_op | source)
XLA Modules:
  0.0 318.8 jit_solution(7484145724764435932)
XLA Ops:
  7.2 4.1 %all_gather.9 = bf16[32,4096]{1,0:T(8,128)(2,1)} all-gather(bf16[32,2048]{1,0:T(8,128)(2,1)} %param.21), channel_id=1, replica_groups=mesh['group'=2,'expert'=8,'cuts'=2] {'cuts'}, dimensions={1}, use_global_device_ids=true | all-gather | bytes 393216 | tf_op jit(solution)/shard_map/all_gather | solution.py:61
  13.2 50.0 %all-gather.2.cloned.1.call-done = bf16[256,4096]{1,0:T(8,128)(2,1)} async-done(((bf16[32,4096]{1,0:T(8,128)(2,1)}), bf16[256,4096]{1,0:T(8,128)(2,1)}) %all-gather.2.cloned.1.call-update) | async-done | bytes 2097168 | tf_op jit(solution)/shard_map/all_gather | solution.py:62
  63.2 2.1 fusion
  65.4 2.4 convolution_bitcast_fusion
  68.4 65.3 %all-reduce.3 = (f32[256,32]{0,1:T(8,128)S(1)}, bf16[256,512]{1,0:T(8,128)(2,1)}) all-reduce(f32[256,32]{0,1:T(8,128)S(1)} %fusion.41, f32[256,512]{1,0:T(8,128)S(1)} %fusion.39), channel_id=1, replica_groups=mesh['group'=2,'expert'=8,'cuts'=2] {'expert','cuts'}, use_global_device_ids=true, to_apply=%region_1.2 | all-reduce | flops 139264 | bytes 851968 | tf_op jit(solution)/shard_map/psum | solution.py:76
  133.8 1.3 fusion.25
  135.9 1.1 slice_multiply_fusion.4
  141.8 2.5 multiply_reduce_fusion
  145.2 1.0 multiply_add_fusion.8
  146.6 3.2 fusion.32
  149.8 2.6 fusion.3
  153.3 69.0 %reduce-scatter.3.cloned.1.call-done = f32[32,2048]{1,0:T(8,128)} async-done(((f32[512,2048]{1,0:T(8,128)}), f32[32,2048]{1,0:T(8,128)}) %reduce-scatter.3.cloned.1.call-update) | async-done | bytes 262160 | tf_op jit(solution)/shard_map/reduce_scatter | solution.py:99
  222.3 1.0 add_convert_fusion
  223.3 2.0 all_gather.11
  226.3 1.4 scatter_custom_fusion
  227.8 29.6 %all_to_all.8 = bf16[8,1,16,4096]{3,2,1,0:T(8,128)(2,1)S(1)} all-to-all(bf16[8,1,16,4096]{3,2,1,0:T(8,128)(2,1)S(1)} %bitcast.143), channel_id=1, replica_groups=mesh['group'=2,'expert'=8,'cuts'=2] {'expert'}, dimensions={0} | all-to-all | bytes 2097152 | tf_op jit(solution)/shard_map/all_to_all | solution.py:123
  257.3 4.5 %fusion.53 = f32[128,768]{1,0:T(8,128)} fusion(bf16[128,4096]{1,0:T(8,128)(2,1)S(1)} %bitcast.139, bf16[4096,768]{1,0:T(8,128)(2,1)} %param.39), kind=kOutput, calls=%fused_computation.141 | convolution fusion | flops 805306368 | bytes 7733248 | tf_op jit(solution)/shard_map/dot_general | solution.py:126
  261.9 8.2 %convolution_convert_fusion = bf16[128,4096]{1,0:T(8,128)(2,1)} fusion(bf16[768,4096]{1,0:T(8,128)(2,1)} %param.41, bf16[128,4096]{1,0:T(8,128)(2,1)S(1)} %bitcast.140, bf16[4096,768]{1,0:T(8,128)(2,1)} %param.40, f32[128,768]{1,0:T(8,128)} %fusion.53), kind=kOutput, calls=%fused_computation.4 | convolution fusion | flops 1611726848 | bytes 15073280 | tf_op jit(solution)/shard_map/dot_general | solution.py:129
  270.0 3.6 %all-to-all-start.1 = ((bf16[1,8,16,4096]{3,2,0,1:T(8,128)(2,1)}), bf16[1,8,16,4096]{3,2,0,1:T(8,128)(2,1)S(1)}, u32[]{:S(2)}, u32[]{:S(2)}) async-start(bf16[1,8,16,4096]{3,2,0,1:T(8,128)(2,1)} %bitcast.141), calls=%async_computation.2 | async-start | bytes 2097152 | tf_op jit(solution)/shard_map/all_to_all | solution.py:131
  273.7 25.5 %all-to-all-done.1 = bf16[1,8,16,4096]{3,2,0,1:T(8,128)(2,1)S(1)} async-done(((bf16[1,8,16,4096]{3,2,0,1:T(8,128)(2,1)}), bf16[1,8,16,4096]{3,2,0,1:T(8,128)(2,1)S(1)}, u32[]{:S(2)}, u32[]{:S(2)}) %all-to-all-start.1) | async-done | bytes 1048608 | tf_op jit(solution)/shard_map/all_to_all | solution.py:131
  300.3 1.2 convert_element_type.97
  301.5 2.1 copy.168
  303.9 6.7 %reduce-scatter.5.cloned.1.call-done = bf16[32,2,2048]{2,0,1:T(8,128)(2,1)} async-done(((bf16[32,2,4096]{2,0,1:T(8,128)(2,1)}), bf16[32,2,2048]{2,0,1:T(8,128)(2,1)}) %reduce-scatter.5.cloned.1.call-update) | async-done | bytes 262160 | tf_op jit(solution)/shard_map/reduce_scatter | solution.py:140
  310.5 1.0 convert_element_type.98
  (79 shorter events, 13.3 us)
Async XLA Ops:
  7.2 58.2 %copy-start = (bf16[4096,256]{1,0:T(8,128)(2,1)S(1)}, bf16[4096,256]{1,0:T(8,128)(2,1)}, u32[]{:S(2)}) copy-start(bf16[4096,256]{1,0:T(8,128)(2,1)} %param.26) | copy-start | bytes 6291460
  7.2 56.0 %all-gather.2.cloned.1.call-start = ((), (), s32[]{:S(2)}) async-start(), calls=%async_computation.4 | async-start | bytes 2359296 | tf_op jit(solution)/shard_map/all_gather | solution.py:62
  11.3 211.0 %reduce-scatter.3.cloned.1.call-start = ((), (), s32[]{:S(2)}) async-start(), calls=%async_computation.5 | async-start | bytes 4456448 | tf_op jit(solution)/shard_map/reduce_scatter | solution.py:99
  13.2 54.6 %copy-start.10 = (f32[256]{0:T(256)S(1)}, f32[256]{0:T(256)}, u32[]{:S(2)}) copy-start(f32[256]{0:T(256)} %param.29) | copy-start | bytes 3076
  63.2 4.8 %copy-start.4 = (bf16[256,512]{1,0:T(8,128)(2,1)S(1)}, bf16[256,512]{1,0:T(8,128)(2,1)}, u32[]{:S(2)}) copy-start(bf16[256,512]{1,0:T(8,128)(2,1)} %param.30) | copy-start | bytes 786436
  65.3 3.0 copy-start.8
  65.4 2.9 copy-start.11
  65.4 68.4 %copy-start.12 = (f32[256]{0:T(256)S(1)}, f32[256]{0:T(256)}, u32[]{:S(2)}) copy-start(f32[256]{0:T(256)} %param.33) | copy-start | bytes 3076
  67.7 73.4 %copy-start.2 = (f32[32,16,256]{2,1,0:T(8,128)S(1)}, f32[32,16,256]{2,1,0:T(8,128)}, u32[]{:S(2)}) copy-start(f32[32,16,256]{2,1,0:T(8,128)} %param.24) | copy-start | bytes 1572868
  67.8 73.4 %copy-start.5 = (f32[16,256]{1,0:T(8,128)S(1)}, f32[16,256]{1,0:T(8,128)}, u32[]{:S(2)}) copy-start(f32[16,256]{1,0:T(8,128)} %param.34) | copy-start | bytes 49156
  146.6 3.2 %copy-start.1 = (bf16[256,4096]{1,0:T(8,128)(2,1)S(1)}, bf16[256,4096]{1,0:T(8,128)(2,1)}, u32[]{:S(2)}) copy-start(bf16[256,4096]{1,0:T(8,128)(2,1)} %param.36) | copy-start | bytes 6291460
  149.8 2.7 copy-start.9
  149.8 72.5 %copy-start.3 = (bf16[32,2048]{1,0:T(8,128)(2,1)S(1)}, bf16[32,2048]{1,0:T(8,128)(2,1)}, u32[]{:S(2)}) copy-start(bf16[32,2048]{1,0:T(8,128)(2,1)} %param.21) | copy-start | bytes 393220
  152.5 73.0 %copy-start.7 = (f32[4096]{0:T(1024)S(1)}, f32[4096]{0:T(1024)}, u32[]{:S(2)}) copy-start(f32[4096]{0:T(1024)} %param.37) | copy-start | bytes 49156
  270.0 29.2 %all-to-all-start.1 = ((bf16[1,8,16,4096]{3,2,0,1:T(8,128)(2,1)}), bf16[1,8,16,4096]{3,2,0,1:T(8,128)(2,1)S(1)}, u32[]{:S(2)}, u32[]{:S(2)}) async-start(bf16[1,8,16,4096]{3,2,0,1:T(8,128)(2,1)} %bitcast.141), calls=%async_computation.2 | async-start | bytes 2097152 | tf_op jit(solution)/shard_map/all_to_all | solution.py:131
  273.7 36.9 %reduce-scatter.5.cloned.1.call-start = ((), (), s32[]{:S(2)}) async-start(), calls=%async_computation.6 | async-start | bytes 786432 | tf_op jit(solution)/shard_map/reduce_scatter | solution.py:140
  299.4 4.2 %copy-start.6 = (bf16[4096,16]{0,1:T(8,128)(2,1)S(1)}, bf16[4096,16]{0,1:T(8,128)(2,1)}, u32[]{:S(2)}) copy-start(bf16[4096,16]{0,1:T(8,128)(2,1)} %param.38) | copy-start | bytes 393220
Sparse Core Ops, SparseCore 0:
  11.5 51.7 all-gather.1
  152.6 69.6 reduce-scatter.2
  303.7 6.7 reduce-scatter.4
where the time goes:
time: 320 us; the launch traced here: 319 us
  waiting for transfers between devices  151 us (47%)
  blocking collectives  101 us (32%)
  matrix products  22.8 us (7%)
  between operations  14.1 us (4%)
  local copies, waits for them, and re-layouts  13.1 us (4%)
  other arithmetic  12.9 us (4%)
  starting transfers between devices  3.76 us (1%)
    reduce_scatter x1, waiting for transfers between devices, on_device(): lax.psum_scatter(term, ('expert', 'cuts'), scatter_dimension=0, tiled=True)  69 us
    psum x1, blocking collectives, on_device(): dt_low, maps = lax.psum((dt_part, map_part), ('expert', 'cuts'))  65.3 us
    all_gather x1, waiting for transfers between devices, on_device(): lax.all_gather(full_x, 'expert', axis=0, tiled=True)  50 us
    all_to_all x1, blocking collectives, on_device(): lax.all_to_all(outgoing, 'expert', split_axis=0, concat_axis=1, tiled=True)  29.6 us
    all_to_all x1, waiting for transfers between devices, on_device(): lax.all_to_all(partial_out.astype(jnp.bfloat16), 'expert', split_axis=1,...  25.5 us
    dot_general x1, matrix products, on_device(): partial_out = jnp.dot(act, w_down, preferred_element_type=jnp.float32)  8.17 us
    reduce_scatter x1, waiting for transfers between devices, on_device(): lax.psum_scatter(picked.astype(jnp.bfloat16), 'cuts', scatter_dimension=2...  6.68 us
  transfers between devices with their start and end apart: 4, of which 4 were waited for; matrix products, arithmetic and copies ran while one was open for 1% of the time, Pallas kernels for 0%

commit v1 on v0

--- a/solution.py
+++ b/solution.py
@@ -6,6 +6,27 @@
 EXPERTS = 2
 DRAFT = 8
 CAP = 16
+
+
+def ring_gather(value, axis, dim):
+    length, mine, rows = (lax.axis_size(axis), lax.axis_index(axis), value.shape[dim])
+    ahead = [(i, (i + 1) % length) for i in range(length)]
+    downward = [(i, (i - 1) % length) for i in range(length)]
+    out = jnp.zeros((*value.shape[:dim], length * rows, *value.shape[dim + 1 :]), value.dtype)
+    out = lax.dynamic_update_slice_in_dim(out, value, mine * rows, axis=dim)
+    from_left = from_right = value
+    half = length // 2
+    for hop in range(1, half + 1):
+        from_left = lax.ppermute(from_left, axis, ahead)
+        out = lax.dynamic_update_slice_in_dim(
+            out, from_left, (mine - hop) % length * rows, axis=dim
+        )
+        if hop < length - half:
+            from_right = lax.ppermute(from_right, axis, downward)
+            out = lax.dynamic_update_slice_in_dim(
+                out, from_right, (mine + hop) % length * rows, axis=dim
+            )
+    return out
 
 
 def rms_norm(values, gain):
@@ -59,7 +80,7 @@
     owners = lax.axis_size("expert")
     pieces = lax.axis_size("cuts")
     full_x = lax.all_gather(x_in, "cuts", axis=1, tiled=True)
-    normed = rms_norm(lax.all_gather(full_x, "expert", axis=0, tiled=True), mamba_gain)
+    normed = rms_norm(ring_gather(full_x, "expert", 0), mamba_gain)
     upper = jnp.dot(normed, in_x, preferred_element_type=jnp.float32)
     lower = jnp.dot(normed, in_z, preferred_element_type=jnp.float32)
     both = jnp.stack([upper, lower])

time: 320 us -> 313 us (0.978)
  waiting for transfers between devices: 151 us -> 124 us
  starting transfers between devices: 3.76 us -> 23.1 us
  local copies, waits for them, and re-layouts: 13.1 us -> 19.1 us
    all_gather x1 -> x0, waiting for transfers between devices: 50 us -> none  [on_device(): lax.all_gather(full_x, 'expert', axis=0, tiled=True)]
    ppermute x0 -> x7, waiting for transfers between devices: none -> 23.5 us  [the longest x4 23.5 us: ring_gather(): from_left = lax.ppermute(from_left, axis, ahead)]
    ppermute x0 -> x7, starting transfers between devices: none -> 19.4 us  [the longest x4 10.3 us: ring_gather(): from_left = lax.ppermute(from_left, axis, ahead)]
    dynamic_update_slice x0 -> x8, local copies, waits for them, and re-layouts: none -> 5.73 us  [the longest x4 2.9 us: ring_gather(): lax.dynamic_update_slice_in_dim(out, from_left, (mine - hop) % length * r...]
  transfers between devices with their start and end apart: 4 -> 10, of which waited for: 4 -> 7; matrix products, arithmetic and copies ran while one was open for 1% -> 2% of each run, Pallas kernels for 0% -> 0%
where the time goes in v1:
time: 313 us
  waiting for transfers between devices  124 us (40%)
  blocking collectives  98.3 us (31%)
  starting transfers between devices  23.1 us (7%)
  matrix products  22.8 us (7%)
  local copies, waits for them, and re-layouts  19.1 us (6%)
  between operations  14.6 us (5%)
  other arithmetic  10.8 us (3%)
    reduce_scatter x1, waiting for transfers between devices, on_device(): lax.psum_scatter(term, ('expert', 'cuts'), scatter_dimension=0, tiled=True)  68.4 us
    psum x1, blocking collectives, on_device(): dt_low, maps = lax.psum((dt_part, map_part), ('expert', 'cuts'))  64.3 us
    all_to_all x1, blocking collectives, on_device(): lax.all_to_all(outgoing, 'expert', split_axis=0, concat_axis=1, tiled=True)  29.5 us
    all_to_all x1, waiting for transfers between devices, on_device(): lax.all_to_all(partial_out.astype(jnp.bfloat16), 'expert', split_axis=1,...  25.5 us
    ppermute x4, waiting for transfers between devices, ring_gather(): from_left = lax.ppermute(from_left, axis, ahead)  23.5 us
    ppermute x4, starting transfers between devices, ring_gather(): from_left = lax.ppermute(from_left, axis, ahead)  10.3 us
    ppermute x3, starting transfers between devices, ring_gather(): from_right = lax.ppermute(from_right, axis, downward)  9.12 us
    dot_general x1, matrix products, on_device(): partial_out = jnp.dot(act, w_down, preferred_element_type=jnp.float32)  8.15 us
  transfers between devices with their start and end apart: 10, of which 7 were waited for; matrix products, arithmetic and copies ran while one was open for 2% of the time, Pallas kernels for 0%

profile of v1, /device:TPU:0, one launch (start us, length us, event | category | flops | bytes accessed | tf_op | source)
XLA Modules:
  0.0 312.8 jit_solution(7064053719413192031)
XLA Ops:
  7.2 2.5 all_gather.6
  9.8 2.9 collective-permute-start
  12.6 3.0 collective-permute-start.1
  18.1 6.1 %collective-permute-done = bf16[32,4096]{1,0:T(8,128)(2,1)S(1)} collective-permute-done((bf16[32,4096]{1,0:T(8,128)(2,1)S(1)}, bf16[32,4096]{1,0:T(8,128)(2,1)S(1)}, u32[]{:S(2)}, u32[]{:S(2)}) %collective-permute-start) | collective-permute-done | bytes 262176 | tf_op jit(solution)/shard_map/ppermute | solution.py:20
  24.2 2.5 collective-permute-start.2
  26.6 3.0 collective-permute-start.3
  31.1 6.2 %collective-permute-done.2 = bf16[32,4096]{1,0:T(8,128)(2,1)S(1)} collective-permute-done((bf16[32,4096]{1,0:T(8,128)(2,1)S(1)}, bf16[32,4096]{1,0:T(8,128)(2,1)S(1)}, u32[]{:S(2)}, u32[]{:S(2)}) %collective-permute-start.2) | collective-permute-done | bytes 262176 | tf_op jit(solution)/shard_map/ppermute | solution.py:20
  37.3 2.5 collective-permute-start.4
  39.8 3.0 collective-permute-start.5
  44.3 5.5 %collective-permute-done.4 = bf16[32,4096]{1,0:T(8,128)(2,1)S(1)} collective-permute-done((bf16[32,4096]{1,0:T(8,128)(2,1)S(1)}, bf16[32,4096]{1,0:T(8,128)(2,1)S(1)}, u32[]{:S(2)}, u32[]{:S(2)}) %collective-permute-start.4) | collective-permute-done | bytes 262176 | tf_op jit(solution)/shard_map/ppermute | solution.py:20
  49.7 2.5 collective-permute-start.6
  53.7 5.8 %collective-permute-done.6 = bf16[32,4096]{1,0:T(8,128)(2,1)S(1)} collective-permute-done((bf16[32,4096]{1,0:T(8,128)(2,1)S(1)}, bf16[32,4096]{1,0:T(8,128)(2,1)S(1)}, u32[]{:S(2)}, u32[]{:S(2)}) %collective-permute-start.6) | collective-permute-done | bytes 262176 | tf_op jit(solution)/shard_map/ppermute | solution.py:20
  62.3 2.4 convolution_bitcast_fusion
  65.4 64.3 %all-reduce.3 = (f32[256,32]{0,1:T(8,128)S(1)}, bf16[256,512]{1,0:T(8,128)(2,1)}) all-reduce(f32[256,32]{0,1:T(8,128)S(1)} %fusion.41, f32[256,512]{1,0:T(8,128)S(1)} %fusion.39), channel_id=1, replica_groups=mesh['group'=2,'expert'=8,'cuts'=2] {'expert','cuts'}, use_global_device_ids=true, to_apply=%region_1.2 | all-reduce | flops 139264 | bytes 851968 | tf_op jit(solution)/shard_map/psum | solution.py:97
  140.4 3.2 %fusion.32 = bf16[256,256]{1,0:T(8,128)(2,1)S(1)} fusion(f32[32,8,256]{2,1,0:T(8,128)S(1)} %stack.2, bf16[4096,256]{1,0:T(8,128)(2,1)} %param.27, bf16[256,4096]{1,0:T(8,128)(2,1)} %constant_dynamic-update-slice_fusion, f32[4096]{0:T(1024)S(1)} %copy-done.20, f32[256]{0:T(256)S(1)} %copy-done.17), kind=kOutput, calls=%fused_computation.67 | convolution fusion | flops 541458432 | bytes 4604928 | tf_op jit(solution)/shard_map/dot_general | solution.py:85
  143.5 2.7 fusion.3
  147.6 68.4 %reduce-scatter.3.cloned.1.call-done = f32[32,2048]{1,0:T(8,128)} async-done(((f32[512,2048]{1,0:T(8,128)}), f32[32,2048]{1,0:T(8,128)}) %reduce-scatter.3.cloned.1.call-update) | async-done | bytes 262160 | tf_op jit(solution)/shard_map/reduce_scatter | solution.py:120
  221.5 29.5 %all_to_all.8 = bf16[8,1,16,4096]{3,2,1,0:T(8,128)(2,1)S(1)} all-to-all(bf16[8,1,16,4096]{3,2,1,0:T(8,128)(2,1)S(1)} %bitcast.143), channel_id=1, replica_groups=mesh['group'=2,'expert'=8,'cuts'=2] {'expert'}, dimensions={0} | all-to-all | bytes 2097152 | tf_op jit(solution)/shard_map/all_to_all | solution.py:144
  251.0 4.5 %fusion.53 = f32[128,768]{1,0:T(8,128)} fusion(bf16[128,4096]{1,0:T(8,128)(2,1)S(1)} %bitcast.139, bf16[4096,768]{1,0:T(8,128)(2,1)} %param.39), kind=kOutput, calls=%fused_computation.149 | convolution fusion | flops 805306368 | bytes 7733248 | tf_op jit(solution)/shard_map/dot_general | solution.py:147
  255.6 8.2 %convolution_convert_fusion = bf16[128,4096]{1,0:T(8,128)(2,1)} fusion(bf16[768,4096]{1,0:T(8,128)(2,1)} %param.41, bf16[128,4096]{1,0:T(8,128)(2,1)S(1)} %bitcast.140, bf16[4096,768]{1,0:T(8,128)(2,1)} %param.40, f32[128,768]{1,0:T(8,128)} %fusion.53), kind=kOutput, calls=%fused_computation.4 | convolution fusion | flops 1611726848 | bytes 15073280 | tf_op jit(solution)/shard_map/dot_general | solution.py:150
  263.7 3.6 %all-to-all-start.1 = ((bf16[1,8,16,4096]{3,2,0,1:T(8,128)(2,1)}), bf16[1,8,16,4096]{3,2,0,1:T(8,128)(2,1)S(1)}, u32[]{:S(2)}, u32[]{:S(2)}) async-start(bf16[1,8,16,4096]{3,2,0,1:T(8,128)(2,1)} %bitcast.141), calls=%async_computation.2 | async-start | bytes 2097152 | tf_op jit(solution)/shard_map/all_to_all | solution.py:152
  267.4 25.5 %all-to-all-done.1 = bf16[1,8,16,4096]{3,2,0,1:T(8,128)(2,1)S(1)} async-done(((bf16[1,8,16,4096]{3,2,0,1:T(8,128)(2,1)}), bf16[1,8,16,4096]{3,2,0,1:T(8,128)(2,1)S(1)}, u32[]{:S(2)}, u32[]{:S(2)}) %all-to-all-start.1) | async-done | bytes 1048608 | tf_op jit(solution)/shard_map/all_to_all | solution.py:152
  295.2 2.1 copy.168
  297.5 6.7 %reduce-scatter.5.cloned.1.call-done = bf16[32,2,2048]{2,0,1:T(8,128)(2,1)} async-done(((bf16[32,2,4096]{2,0,1:T(8,128)(2,1)}), bf16[32,2,2048]{2,0,1:T(8,128)(2,1)}) %reduce-scatter.5.cloned.1.call-update) | async-done | bytes 262160 | tf_op jit(solution)/shard_map/reduce_scatter | solution.py:161
  (117 shorter events, 31.7 us)
Async XLA Ops:
  7.2 55.1 %copy-start = (bf16[4096,256]{1,0:T(8,128)(2,1)S(1)}, bf16[4096,256]{1,0:T(8,128)(2,1)}, u32[]{:S(2)}) copy-start(bf16[4096,256]{1,0:T(8,128)(2,1)} %param.26) | copy-start | bytes 6291460
  7.2 10.8 %copy-start.7 = (f32[32,3,256]{2,0,1:T(8,128)S(1)}, f32[32,3,256]{2,0,1:T(8,128)}, u32[]{:S(2)}) copy-start(f32[32,3,256]{2,0,1:T(8,128)} %param.23) | copy-start | bytes 294916
  7.2 10.9 %copy-start.13 = (f32[4,256]{1,0:T(4,128)S(1)}, f32[4,256]{1,0:T(4,128)}, u32[]{:S(2)}) copy-start(f32[4,256]{1,0:T(4,128)} %param.28) | copy-start | bytes 12292
  7.2 208.8 %reduce-scatter.3.cloned.1.call-start = ((), (), s32[]{:S(2)}) async-start(), calls=%async_computation.4 | async-start | bytes 4456448 | tf_op jit(solution)/shard_map/reduce_scatter | solution.py:120
  9.8 14.4 %collective-permute-start = (bf16[32,4096]{1,0:T(8,128)(2,1)S(1)}, bf16[32,4096]{1,0:T(8,128)(2,1)S(1)}, u32[]{:S(2)}, u32[]{:S(2)}) collective-permute-start(bf16[32,4096]{1,0:T(8,128)(2,1)S(1)} %all_gather.6), channel_id=1, source_target_pairs={{0,2},{2,4},{4,6},{6,8},{8,10},{10,12},{12,14},{14,0},{1,3},{3,5},... | collective-permute-start | bytes 786440 | tf_op jit(solution)/shard_map/ppermute | solution.py:20
  12.6 14.0 %collective-permute-start.1 = (bf16[32,4096]{1,0:T(8,128)(2,1)S(1)}, bf16[32,4096]{1,0:T(8,128)(2,1)S(1)}, u32[]{:S(2)}, u32[]{:S(2)}) collective-permute-start(bf16[32,4096]{1,0:T(8,128)(2,1)S(1)} %all_gather.6), channel_id=1, source_target_pairs={{0,14},{2,0},{4,2},{6,4},{8,6},{10,8},{12,10},{14,12},{1,15},{3,1}... | collective-permute-start | bytes 786440 | tf_op jit(solution)/shard_map/ppermute | solution.py:25
  24.2 13.2 %collective-permute-start.2 = (bf16[32,4096]{1,0:T(8,128)(2,1)S(1)}, bf16[32,4096]{1,0:T(8,128)(2,1)S(1)}, u32[]{:S(2)}, u32[]{:S(2)}) collective-permute-start(bf16[32,4096]{1,0:T(8,128)(2,1)S(1)} %collective-permute-done), channel_id=1, source_target_pairs={{0,2},{2,4},{4,6},{6,8},{8,10},{10,12},{12,14},{14,0},{1,3},{3,5},... | collective-permute-start | bytes 786440 | tf_op jit(solution)/shard_map/ppermute | solution.py:20
  26.6 13.2 %collective-permute-start.3 = (bf16[32,4096]{1,0:T(8,128)(2,1)S(1)}, bf16[32,4096]{1,0:T(8,128)(2,1)S(1)}, u32[]{:S(2)}, u32[]{:S(2)}) collective-permute-start(bf16[32,4096]{1,0:T(8,128)(2,1)S(1)} %collective-permute-done.1), channel_id=1, source_target_pairs={{0,14},{2,0},{4,2},{6,4},{8,6},{10,8},{12,10},{14,12},{1,15},{3,1}... | collective-permute-start | bytes 786440 | tf_op jit(solution)/shard_map/ppermute | solution.py:25
  37.3 12.4 %collective-permute-start.4 = (bf16[32,4096]{1,0:T(8,128)(2,1)S(1)}, bf16[32,4096]{1,0:T(8,128)(2,1)S(1)}, u32[]{:S(2)}, u32[]{:S(2)}) collective-permute-start(bf16[32,4096]{1,0:T(8,128)(2,1)S(1)} %collective-permute-done.2), channel_id=1, source_target_pairs={{0,2},{2,4},{4,6},{6,8},{8,10},{10,12},{12,14},{14,0},{1,3},{3,5},... | collective-permute-start | bytes 786440 | tf_op jit(solution)/shard_map/ppermute | solution.py:20
  39.8 13.2 %collective-permute-start.5 = (bf16[32,4096]{1,0:T(8,128)(2,1)S(1)}, bf16[32,4096]{1,0:T(8,128)(2,1)S(1)}, u32[]{:S(2)}, u32[]{:S(2)}) collective-permute-start(bf16[32,4096]{1,0:T(8,128)(2,1)S(1)} %collective-permute-done.3), channel_id=1, source_target_pairs={{0,14},{2,0},{4,2},{6,4},{8,6},{10,8},{12,10},{14,12},{1,15},{3,1}... | collective-permute-start | bytes 786440 | tf_op jit(solution)/shard_map/ppermute | solution.py:25
  43.6 18.7 %copy-start.19 = (f32[4096]{0:T(1024)S(1)}, f32[4096]{0:T(1024)}, u32[]{:S(2)}) copy-start(f32[4096]{0:T(1024)} %param.25) | copy-start | bytes 49156
  49.7 9.7 %collective-permute-start.6 = (bf16[32,4096]{1,0:T(8,128)(2,1)S(1)}, bf16[32,4096]{1,0:T(8,128)(2,1)S(1)}, u32[]{:S(2)}, u32[]{:S(2)}) collective-permute-start(bf16[32,4096]{1,0:T(8,128)(2,1)S(1)} %collective-permute-done.4), channel_id=1, source_target_pairs={{0,2},{2,4},{4,6},{6,8},{8,10},{10,12},{12,14},{14,0},{1,3},{3,5},... | collective-permute-start | bytes 786440 | tf_op jit(solution)/shard_map/ppermute | solution.py:20
  64.7 65.0 %copy-start.18 = (bf16[512,256]{1,0:T(8,128)(2,1)S(1)}, bf16[512,256]{1,0:T(8,128)(2,1)}, u32[]{:S(2)}) copy-start(bf16[512,256]{1,0:T(8,128)(2,1)} %param.32) | copy-start | bytes 786436
  64.7 64.9 %copy-start.21 = (f32[256]{0:T(256)S(1)}, f32[256]{0:T(256)}, u32[]{:S(2)}) copy-start(f32[256]{0:T(256)} %param.33) | copy-start | bytes 3076
  129.7 6.5 %copy-start.2 = (f32[32,16,256]{2,1,0:T(8,128)S(1)}, f32[32,16,256]{2,1,0:T(8,128)}, u32[]{:S(2)}) copy-start(f32[32,16,256]{2,1,0:T(8,128)} %param.24) | copy-start | bytes 1572868
  129.7 6.5 %copy-start.5 = (f32[16,256]{1,0:T(8,128)S(1)}, f32[16,256]{1,0:T(8,128)}, u32[]{:S(2)}) copy-start(f32[16,256]{1,0:T(8,128)} %param.34) | copy-start | bytes 49156
  136.2 3.4 %copy-start.15 = (f32[256]{0:T(256)S(1)}, f32[256]{0:T(256)}, u32[]{:S(2)}) copy-start(f32[256]{0:T(256)} %param.35) | copy-start | bytes 3076
  136.9 3.4 %copy-start.17 = (f32[256]{0:T(256)S(1)}, f32[256]{0:T(256)}, u32[]{:S(2)}) copy-start(f32[256]{0:T(256)} %copy-done.16) | copy-start | bytes 3076
  136.9 3.4 %copy-start.20 = (f32[4096]{0:T(1024)S(1)}, f32[4096]{0:T(1024)}, u32[]{:S(2)}) copy-start(f32[4096]{0:T(1024)} %param.25) | copy-start | bytes 49156
  146.2 69.8 %copy-start.3 = (bf16[32,2048]{1,0:T(8,128)(2,1)S(1)}, bf16[32,2048]{1,0:T(8,128)(2,1)}, u32[]{:S(2)}) copy-start(bf16[32,2048]{1,0:T(8,128)(2,1)} %param.21) | copy-start | bytes 393220
  146.2 73.0 %copy-start.10 = (f32[4096]{0:T(1024)S(1)}, f32[4096]{0:T(1024)}, u32[]{:S(2)}) copy-start(f32[4096]{0:T(1024)} %param.37) | copy-start | bytes 49156
  263.7 29.2 %all-to-all-start.1 = ((bf16[1,8,16,4096]{3,2,0,1:T(8,128)(2,1)}), bf16[1,8,16,4096]{3,2,0,1:T(8,128)(2,1)S(1)}, u32[]{:S(2)}, u32[]{:S(2)}) async-start(bf16[1,8,16,4096]{3,2,0,1:T(8,128)(2,1)} %bitcast.141), calls=%async_computation.2 | async-start | bytes 2097152 | tf_op jit(solution)/shard_map/all_to_all | solution.py:152
  267.4 36.8 %reduce-scatter.5.cloned.1.call-start = ((), (), s32[]{:S(2)}) async-start(), calls=%async_computation.5 | async-start | bytes 786432 | tf_op jit(solution)/shard_map/reduce_scatter | solution.py:161
  294.0 3.3 %copy-start.6 = (bf16[4096,16]{0,1:T(8,128)(2,1)S(1)}, bf16[4096,16]{0,1:T(8,128)(2,1)}, u32[]{:S(2)}) copy-start(bf16[4096,16]{0,1:T(8,128)(2,1)} %param.38) | copy-start | bytes 393220
  (8 other events, 19.4 us)
Sparse Core Ops, SparseCore 0:
  146.4 69.6 reduce-scatter.2
  297.4 6.7 reduce-scatter.4
